TPU v7x, 256 devices: a whole 4x4x8 slice. The times are simulated.
256 devices in a mesh: dp: 8 (over z), space: 8 (over x, core), tensor: 4 (over y).
Axes of the slice: x: 4, y: 4, z: 8, core: 2. Of those that a mesh axis runs over, the one named last changes fastest.
Arguments:
- feat_policy: bfloat16 [8, 2, 320, 32, 128], P('dp', None, 'tensor', 'space'), may hold values from -6 to 6
- feat_ref: bfloat16 [8, 2, 320, 32, 128], P('dp', None, 'tensor', 'space'), may hold values from -6 to 6
- noise: float32 [8, 2, 4, 32, 128], P('dp', None, None, 'space'), may hold values from -6 to 6
- w1_policy: bfloat16 [9, 320, 320], P(None, 'tensor'), may hold values from -0.109375 to 0.109375
- w1_ref: bfloat16 [9, 320, 320], P(None, 'tensor'), may hold values from -0.109375 to 0.109375
- b1_policy: float32 [320], P('tensor'), may hold values from -3 to 3
- b1_ref: float32 [320], P('tensor'), may hold values from -3 to 3
- gn_gain_policy: float32 [320], P('tensor'), may hold values from 0.25 to 1.75
- gn_bias_policy: float32 [320], P('tensor'), may hold values from -3 to 3
- gn_gain_ref: float32 [320], P('tensor'), may hold values from 0.25 to 1.75
- gn_bias_ref: float32 [320], P('tensor'), may hold values from -3 to 3
- w2_policy: bfloat16 [9, 4, 320], P(None, None, 'tensor'), may hold values from -0.109375 to 0.109375
- w2_ref: bfloat16 [9, 4, 320], P(None, None, 'tensor'), may hold values from -0.109375 to 0.109375
- time_table: float32 [1000, 320], P(None, 'tensor'), may hold values from -3 to 3
- timestep: int32 [8], P('dp'), may hold values from 0 to 999
- winner: int32 [8], P('dp'), may hold values from 0 to 1
Outputs:
- logits: float32 [8], P('dp')
- grad_w1: float32 [9, 320, 320], P(None, 'tensor', ('dp', 'space'))
- grad_w2: float32 [9, 4, 320], P(None, None, 'tensor')
All inputs are finite; a program needn't handle non-finite values.
Results may differ from a plain program's by a relative error of at most 0.0068.
Values may be sent and summed in bfloat16 or wider, within the bound.
No kernel may reach another device: no remote copies, remote signals or barrier semaphores. Data moves between devices by JAX's collectives and lax.ppermute only.
A program may use at most 64 MiB of HBM per device.

v0:
```python
import jax
import jax.numpy as jnp
from jax import lax
from jax.sharding import PartitionSpec as P

C = 320
GROUPS = 32
dpo_beta = 500.0
norm_eps = 1e-05


def with_halo(cells, sides, width):
    for axis, dim in sides:
        count = lax.axis_size(axis)
        ends = count - 1
        head = lax.slice_in_dim(cells, 0, width, axis=dim)
        tail = lax.slice_in_dim(cells, cells.shape[dim] - width, cells.shape[dim], axis=dim)
        cells = jnp.concatenate(
            [
                lax.ppermute(tail, axis, [(i, (i + 1) % count) for i in range(ends)]),
                cells,
                lax.ppermute(head, axis, [((i + 1) % count, i) for i in range(ends)]),
            ],
            axis=dim,
        )
    return cells


def to_kernel(weights):
    return weights.reshape(3, 3, weights.shape[1], weights.shape[2]).transpose(2, 3, 0, 1)


def flip_kernel(weights):
    shaped = weights.reshape(3, 3, weights.shape[1], weights.shape[2])[::-1, ::-1]
    return shaped.transpose(3, 2, 0, 1)


def conv_rows(inputs, kernel):
    return lax.conv_general_dilated(
        inputs,
        kernel,
        (1, 1),
        ((0, 0), (1, 1)),
        dimension_numbers=("NCHW", "OIHW", "NCHW"),
        preferred_element_type=jnp.float32,
    )


def kernel_grad(inputs, deltas):
    return lax.conv_general_dilated(
        inputs,
        deltas,
        (1, 1),
        ((0, 0), (1, 1)),
        dimension_numbers=("CNHW", "IOHW", "NCHW"),
        preferred_element_type=jnp.float32,
    )


def group_total(values, group_size):
    local_groups = values.shape[-3] // group_size
    shaped = values.reshape(values.shape[:-3] + (local_groups, group_size) + values.shape[-2:])
    return jnp.sum(shaped, axis=(-3, -2, -1))


def spread_back(stat, group_size):
    return jnp.repeat(stat, group_size, axis=-1)[..., None, None]


def body(
    feat_policy,
    feat_ref,
    noise,
    w1_policy,
    w1_ref,
    b1_policy,
    b1_ref,
    gn_gain_policy,
    gn_bias_policy,
    gn_gain_ref,
    gn_bias_ref,
    w2_policy,
    w2_ref,
    time_table,
    timestep,
    winner,
):
    pair_count = feat_policy.shape[0]
    chan_local = feat_policy.shape[2]
    row_count = feat_policy.shape[3]
    col_count = feat_policy.shape[4]
    latent_chans = noise.shape[2]
    images = 2 * pair_count
    group_size = C // GROUPS
    stacked = jnp.stack(
        [
            feat_policy.reshape(images, chan_local, row_count, col_count),
            feat_ref.reshape(images, chan_local, row_count, col_count),
        ]
    )
    stacked_ext = with_halo(stacked, (("space", 3),), 1)
    onehot = (
        timestep[:, None] == jnp.arange(time_table.shape[0], dtype=jnp.int32)[None, :]
    ).astype(jnp.float32)
    shift = jnp.repeat(jnp.dot(onehot, time_table, precision=lax.Precision.HIGHEST), 2, axis=0)
    kernel_policy = to_kernel(w1_policy)
    kernel_frozen = to_kernel(w1_ref)
    zeros = jnp.zeros((images, chan_local, row_count, col_count), jnp.float32)
    block_in = lax.all_gather(stacked_ext, "tensor", axis=2, tiled=True)
    pre_policy = zeros + conv_rows(block_in[0], kernel_policy)
    pre_frozen = zeros + conv_rows(block_in[1], kernel_frozen)
    pre_policy = pre_policy + (b1_policy[None, :] + shift)[:, :, None, None]
    pre_frozen = pre_frozen + (b1_ref[None, :] + shift)[:, :, None, None]
    pre_both = jnp.stack([pre_policy, pre_frozen])
    group_count = group_size * row_count * lax.axis_size("space") * col_count
    sum_values, sum_squares = lax.psum(
        (group_total(pre_both, group_size), group_total(pre_both * pre_both, group_size)), "space"
    )
    group_mean = sum_values / group_count
    inv_std = lax.rsqrt(sum_squares / group_count - group_mean * group_mean + norm_eps)
    centered = (pre_both - spread_back(group_mean, group_size)) * spread_back(inv_std, group_size)
    gains = jnp.stack([gn_gain_policy, gn_gain_ref])[:, None, :, None, None]
    offsets = jnp.stack([gn_bias_policy, gn_bias_ref])[:, None, :, None, None]
    normed = centered * gains + offsets
    hidden = jax.nn.silu(normed).astype(jnp.bfloat16)
    hidden_ext = with_halo(hidden, (("space", 3),), 1)
    part_policy = conv_rows(hidden_ext[0], to_kernel(w2_policy))
    part_frozen = conv_rows(hidden_ext[1], to_kernel(w2_ref))
    noise_img = noise.reshape(images, latent_chans, row_count, col_count)
    cell_total = latent_chans * row_count * lax.axis_size("space") * col_count
    share_policy, share_frozen = (
        lax.psum_scatter(part_policy, "tensor", scatter_dimension=1, tiled=True),
        lax.psum_scatter(part_frozen, "tensor", scatter_dimension=1, tiled=True),
    )
    per_share = latent_chans // lax.axis_size("tensor")
    noise_own = lax.dynamic_slice_in_dim(
        noise_img, lax.axis_index("tensor") * per_share, per_share, 1
    )
    squares = jnp.stack(
        [
            jnp.sum((share_policy - noise_own) ** 2, axis=(1, 2, 3)),
            jnp.sum((share_frozen - noise_own) ** 2, axis=(1, 2, 3)),
        ]
    )
    errors = lax.psum(squares, ("space", "tensor"))
    residual = share_policy - noise_own
    errors = (errors / cell_total).reshape(2, pair_count, 2)
    pair_sign = 1.0 - 2.0 * winner.astype(jnp.float32)
    logits = (
        -0.5
        * dpo_beta
        * pair_sign
        * (errors[0, :, 0] - errors[0, :, 1] - (errors[1, :, 0] - errors[1, :, 1]))
    )
    weight = jax.nn.sigmoid(-logits)
    scaled = (
        (dpo_beta * weight * pair_sign / cell_total)[:, None]
        * jnp.array([1.0, -1.0], jnp.float32)[None, :]
    ).reshape(images)
    dpred = (scaled[:, None, None, None] * residual).astype(jnp.bfloat16)
    dpred = lax.all_gather(dpred, "tensor", axis=1, tiled=True)
    dpred_ext = with_halo(dpred, (("space", 2),), 1)
    head_local = kernel_grad(hidden_ext[0], dpred)
    head_local = head_local.transpose(2, 3, 1, 0).reshape(9, latent_chans, chan_local)
    grad_w2 = lax.psum(head_local, ("dp", "space"))
    dhidden = conv_rows(dpred_ext, flip_kernel(w2_policy))
    normed_policy = normed[0]
    centered_policy = centered[0]
    gate_value = jax.nn.sigmoid(normed_policy)
    gnorm = (
        dhidden
        * gate_value
        * (1.0 + normed_policy * (1.0 - gate_value))
        * gn_gain_policy[None, :, None, None]
    )
    first_sum, second_sum = lax.psum(
        (group_total(gnorm, group_size), group_total(gnorm * centered_policy, group_size)), "space"
    )
    first_mean = spread_back(first_sum / group_count, group_size)
    second_mean = spread_back(second_sum / group_count, group_size)
    delta = (
        spread_back(inv_std[0], group_size) * (gnorm - first_mean - centered_policy * second_mean)
    ).astype(jnp.bfloat16)
    body_local = kernel_grad(lax.all_gather(stacked_ext[0], "tensor", axis=1, tiled=True), delta)
    body_local = body_local.transpose(2, 3, 1, 0).reshape(9, chan_local, body_local.shape[0])
    grad_w1 = lax.psum_scatter(body_local, ("dp", "space"), scatter_dimension=2, tiled=True)
    return (logits, grad_w1, grad_w2)


def solution(mesh):
    in_specs = (
        P("dp", None, "tensor", "space", None),
        P("dp", None, "tensor", "space", None),
        P("dp", None, None, "space", None),
        P(None, "tensor", None),
        P(None, "tensor", None),
        P("tensor"),
        P("tensor"),
        P("tensor"),
        P("tensor"),
        P("tensor"),
        P("tensor"),
        P(None, None, "tensor"),
        P(None, None, "tensor"),
        P(None, "tensor"),
        P("dp"),
        P("dp"),
    )
    out_specs = (P("dp"), P(None, "tensor", ("dp", "space")), P(None, None, "tensor"))
    return jax.shard_map(body, mesh=mesh, in_specs=in_specs, out_specs=out_specs, check_vma=False)
```

profile of v0, /device:TPU:8, one launch (start us, length us, event | category | flops | bytes accessed | tf_op | source)
XLA Modules:
  0.0 516.6 jit_solution(16194882127117866804)
XLA Ops:
  7.3 1.2 copy_dynamic-update-slice_fusion.1
  8.5 1.1 copy_dynamic-update-slice_fusion
  9.8 1.7 collective-permute-start
  11.5 1.3 collective-permute-start.1
  12.8 3.1 collective-permute-done.1
  16.0 1.5 pad_maximum_fusion.2
  18.9 0.6 dynamic-slice.1
  19.6 0.2 fusion.70
  19.8 1.9 slice.99
  21.6 32.6 %all-gather.3.cloned.1.call-done = bf16[2,2,320,6,128]{4,1,3,0,2:T(2,128)(2,1)} async-done(((bf16[2,2,80,6,128]{4,1,3,0,2:T(2,128)(2,1)}), bf16[2,2,320,6,128]{4,1,3,0,2:T(2,128)(2,1)}) %all-gather.3.cloned.1.call-update) | async-done | bytes 1966096 | tf_op jit(solution)/shard_map/all_gather | solution.py:109
  54.3 3.3 slice_bitcast_fusion.1
  57.6 3.8 copy.156
  61.4 1.0 pad.clone
  62.5 1.4 fusion.2
  63.9 2.1 fusion.13
  66.1 0.2 copy.125
  66.3 2.0 copy.157
  68.3 1.0 pad.2.clone
  69.5 1.4 fusion.3
  70.9 2.1 fusion.19
  73.0 0.2 copy.129
  73.3 1.1 copy_bitcast_fusion.1
  74.3 0.2 copy.131
  74.6 0.2 copy.132
  74.8 0.4 fusion.43
  75.2 14.6 %all-reduce.4 = (f32[2,2,8]{2,1,0:T(2,128)S(1)}, f32[2,2,8]{2,1,0:T(2,128)S(1)}) all-reduce(f32[2,2,8]{2,1,0:T(2,128)S(1)} %get-tuple-element.4, f32[2,2,8]{2,1,0:T(2,128)S(1)} %get-tuple-element.3), channel_id=1, replica_groups=mesh['dp'=8,'space'=8,'tensor'=4] {'space'}, use_global_device_ids=true, to_apply=%region_3.0 | all-reduce | flops 64 | bytes 512 | tf_op jit(solution)/shard_map/psum | solution.py:116
  90.1 2.5 fusion.25
  92.6 0.2 fusion.66
  92.8 1.3 collective-permute-start.2
  94.1 1.3 collective-permute-start.3
  95.4 14.1 %all-gather = bf16[1,2,320,6,128]{4,1,3,0,2:T(2,128)(2,1)S(1)} all-gather(bf16[1,2,80,6,128]{4,1,3,0,2:T(2,128)(2,1)S(1)} %copy-done.2), channel_id=2, replica_groups=mesh['dp'=8,'space'=8,'tensor'=4] {'tensor'}, dimensions={2}, use_global_device_ids=true | all-gather | bytes 1228800 | tf_op jit(solution)/shard_map/all_gather | solution.py:184
  109.5 1.4 pad_maximum_fusion
  110.9 1.3 slice_bitcast_fusion.4
  112.2 0.4 pad.6
  112.7 4.0 convolution_select_fusion.1
  116.7 1.1 copy.139
  117.9 1.4 pad.4
  119.4 4.7 convolution_select_fusion.2
  124.1 1.1 copy.135
  125.4 15.8 %all-reduce.5 = (f32[2,4,4,128]{3,2,0,1:T(4,128)S(1)}, f32[2,4,4,128]{3,2,0,1:T(4,128)S(1)}) all-reduce(f32[2,4,4,128]{3,2,0,1:T(4,128)S(1)} %copy.136, f32[2,4,4,128]{3,2,0,1:T(4,128)S(1)} %copy.140), channel_id=3, replica_groups=mesh['dp'=8,'space'=8,'tensor'=4] {'tensor'}, use_global_device_ids=true, to_apply=%region_4.5.clone | all-reduce | flops 8192 | bytes 65536
  141.1 1.4 multiply_reduce_fusion.2
  142.6 3.2 copy.141
  145.8 64.8 %psum.44 = f32[2,2]{1,0:T(2,128)S(1)} all-reduce(f32[2,2]{1,0:T(2,128)S(1)} %pad_maximum_fusion.5), channel_id=1, replica_groups=mesh['dp'=8,'space'=8,'tensor'=4] {'space','tensor'}, use_global_device_ids=true, to_apply=%region_8.9 | all-reduce | flops 4 | bytes 32 | tf_op jit(solution)/shard_map/psum | solution.py:145
  210.6 0.7 fusion.69
  213.9 0.7 broadcast_multiply_fusion.3
  214.5 1.4 multiply_convert_fusion.2
  215.9 10.2 %all_gather.11 = bf16[2,4,4,128]{3,2,0,1:T(4,128)(2,1)S(1)} all-gather(bf16[2,1,4,128]{3,2,0,1:T(4,128)(2,1)S(1)} %multiply_convert_fusion.2), channel_id=1, replica_groups=mesh['dp'=8,'space'=8,'tensor'=4] {'tensor'}, dimensions={1}, use_global_device_ids=true | all-gather | bytes 10240 | tf_op jit(solution)/shard_map/all_gather | solution.py:161
  226.1 1.3 collective-permute-start.4
  227.4 1.3 collective-permute-start.5
  228.9 1.6 collective-permute-done.5
  230.6 0.1 reshape.113
  230.9 0.2 copy.146
  231.2 0.4 convolution_select_fusion
  231.6 0.2 copy.147
  231.9 0.9 copy-done.1
  232.8 1.4 fusion.63
  234.5 12.8 %all-reduce.3 = (f32[2,8]{1,0:T(2,128)S(1)}, f32[2,8]{1,0:T(2,128)S(1)}) all-reduce(f32[2,8]{1,0:T(2,128)S(1)} %reduce_sum.77, f32[2,8]{1,0:T(2,128)S(1)} %reduce_sum.74), channel_id=1, replica_groups=mesh['dp'=8,'space'=8,'tensor'=4] {'space'}, use_global_device_ids=true, to_apply=%region_14.15 | all-reduce | flops 32 | bytes 256 | tf_op jit(solution)/shard_map/psum | solution.py:176
  247.6 7.1 %fusion.22 = f32[3,3,80,320]{2,3,1,0:T(8,128)} fusion(bf16[1,2,320,6,128]{2,1,4,3,0:T(2,128)(2,1)} %copy.141, f32[2,80,4,128]{1,0,3,2:T(2,128)S(1)} %get-tuple-element.15, f32[2,2,80,4,128]{2,1,4,3,0:T(2,128)S(1)} %get-tuple-element.18, f32[2,80]{1,0:T(2,128)S(1)} %mul.129, f32[2,80]{1,0:T(2,128)S(1)} %sub.65, f32[2,80]{1,0:T(2,128)S(1)} %mul.114), kind=kOutput, calls=%fused_computation.16 | convolution fusion | flops 469811200 | bytes 2956288 | tf_op jit(solution)/shard_map/transpose | solution.py:185
  254.8 0.7 copy-done.14
  255.4 0.6 dynamic-slice.5
  256.6 0.3 copy.150
  257.0 1.6 fusion.44
  258.6 248.5 %psum.47 = f32[9,4,80]{2,1,0:T(4,128)} all-reduce(f32[9,4,80]{2,1,0:T(4,128)S(1)} %bitcast.159), channel_id=1, replica_groups=mesh['dp'=8,'space'=8,'tensor'=4] {'dp','space'}, use_global_device_ids=true, to_apply=%region_16.17 | all-reduce | flops 2880 | bytes 23040 | tf_op jit(solution)/shard_map/psum | solution.py:165
  507.1 1.5 constant_dynamic-slice_fusion
  (91 shorter events, 2.5 us)
Async XLA Ops:
  7.2 56.8 %copy-start = (bf16[9,80,320]{2,1,0:T(8,128)(2,1)S(1)}, bf16[9,80,320]{2,1,0:T(8,128)(2,1)}, u32[]{:S(2)}) copy-start(bf16[9,80,320]{2,1,0:T(8,128)(2,1)} %param.20) | copy-start | bytes 1382404
  7.2 11.7 %copy-start.15 = (u32[256]{0:T(256)S(1)}, u32[256]{0:T(256)}, u32[]{:S(2)}) copy-start(u32[256]{0:T(256)} %constant.73) | copy-start | bytes 3076
  7.2 12.3 %copy-start.4 = (f32[80]{0:T(128)S(1)}, f32[80]{0:T(128)}, u32[]{:S(2)}) copy-start(f32[80]{0:T(128)} %param.24) | copy-start | bytes 964
  7.2 12.3 %copy-start.8 = (f32[80]{0:T(128)S(1)}, f32[80]{0:T(128)}, u32[]{:S(2)}) copy-start(f32[80]{0:T(128)} %param.26) | copy-start | bytes 964
  7.2 12.3 %copy-start.10 = (f32[80]{0:T(128)S(1)}, f32[80]{0:T(128)}, u32[]{:S(2)}) copy-start(f32[80]{0:T(128)} %param.25) | copy-start | bytes 964
  7.2 12.3 %copy-start.9 = (f32[80]{0:T(128)S(1)}, f32[80]{0:T(128)}, u32[]{:S(2)}) copy-start(f32[80]{0:T(128)} %param.27) | copy-start | bytes 964
  7.2 12.3 %copy-start.6 = (f32[80]{0:T(128)S(1)}, f32[80]{0:T(128)}, u32[]{:S(2)}) copy-start(f32[80]{0:T(128)} %param.22) | copy-start | bytes 964
  7.2 12.3 %copy-start.7 = (f32[80]{0:T(128)S(1)}, f32[80]{0:T(128)}, u32[]{:S(2)}) copy-start(f32[80]{0:T(128)} %param.23) | copy-start | bytes 964
  7.3 12.3 %copy-start.3 = (f32[1000,80]{0,1:T(8,128)S(1)}, f32[1000,80]{0,1:T(8,128)}, u32[]{:S(2)}) copy-start(f32[1000,80]{0,1:T(8,128)} %param.30) | copy-start | bytes 960004
  7.3 47.0 %all-gather.3.cloned.1.call-start = ((), (), s32[]{:S(2)}) async-start(), calls=%async_computation | async-start | bytes 2457600 | tf_op jit(solution)/shard_map/all_gather | solution.py:109
  9.8 3.1 collective-permute-start
  11.5 4.4 collective-permute-start.1
  17.5 489.6 %all-reduce.8.cloned.1.call-start = ((), (), s32[]{:S(2)}) async-start(), calls=%async_computation.1 | async-start | bytes 2949120
  62.5 1.4 copy-start.16
  69.5 1.4 copy-start.11
  90.1 5.3 %copy-start.2 = (bf16[1,2,80,6,128]{4,1,3,0,2:T(2,128)(2,1)S(1)}, bf16[1,2,80,6,128]{4,1,3,0,2:T(2,128)(2,1)}, u32[]{:S(2)}) copy-start(bf16[1,2,80,6,128]{4,1,3,0,2:T(2,128)(2,1)} %slice.99) | copy-start | bytes 737284
  92.8 16.7 %collective-permute-start.2 = (bf16[2,2,80,1,128]{2,1,4,3,0:T(2,128)(2,1)S(1)}, bf16[2,2,80,1,128]{2,1,4,3,0:T(2,128)(2,1)S(1)}, u32[]{:S(2)}, u32[]{:S(2)}) collective-permute-start(bf16[2,2,80,1,128]{2,1,4,3,0:T(2,128)(2,1)S(1)} %get-tuple-element.23), channel_id=1, source_target_pairs={{0,4},{4,8},{8,12},{12,16},{16,20},{20,24},{24,28},{1,5},{5,9},{9,... | collective-permute-start | bytes 245768 | tf_op jit(solution)/shard_map/ppermute | solution.py:20
  94.1 15.4 %collective-permute-start.3 = (bf16[2,2,80,1,128]{2,1,4,3,0:T(2,128)(2,1)S(1)}, bf16[2,2,80,1,128]{2,1,4,3,0:T(2,128)(2,1)S(1)}, u32[]{:S(2)}, u32[]{:S(2)}) collective-permute-start(bf16[2,2,80,1,128]{2,1,4,3,0:T(2,128)(2,1)S(1)} %get-tuple-element.24), channel_id=1, source_target_pairs={{4,0},{8,4},{12,8},{16,12},{20,16},{24,20},{28,24},{5,1},{9,5},{13... | collective-permute-start | bytes 245768 | tf_op jit(solution)/shard_map/ppermute | solution.py:22
  110.9 1.8 copy-start.12
  142.6 88.6 %copy-start.13 = (bf16[9,4,80]{2,1,0:T(4,128)(2,1)S(1)}, bf16[9,4,80]{2,1,0:T(4,128)(2,1)}, u32[]{:S(2)}) copy-start(bf16[9,4,80]{2,1,0:T(4,128)(2,1)} %param.28) | copy-start | bytes 17284
  142.6 88.6 %copy-start.17 = (pred[16,17]{0,1:T(8,128)(4,1)S(1)}, pred[16,17]{0,1:T(8,128)(4,1)}, u32[]{:S(2)}) copy-start(pred[16,17]{0,1:T(8,128)(4,1)} %constant.66) | copy-start | bytes 820
  226.1 2.8 collective-permute-start.4
  227.4 3.1 collective-permute-start.5
  231.6 1.2 copy-start.1
  231.6 1.2 copy-start.5
  254.7 0.7 copy-start.14
Sparse Core Ops, SparseCore 0:
  17.6 36.5 all-gather.2
  254.9 188.4 all-reduce.7
where the time goes:
time: 518 us; the launch traced here: 517 us
  blocking collectives  381 us (74%)
  waiting for transfers between devices  37.4 us (7%)
  local copies, waits for them, and re-layouts  33.8 us (7%)
  matrix products  22.3 us (4%)
  between operations  20.4 us (4%)
  other arithmetic  13.8 us (3%)
  starting transfers between devices  8.29 us (2%)
    psum x1, blocking collectives, body(): grad_w2 = lax.psum(head_local, ('dp', 'space'))  249 us
    psum x1, blocking collectives, body(): errors = lax.psum(squares, ('space', 'tensor'))  64.8 us
    all_gather x1, waiting for transfers between devices, body(): block_in = lax.all_gather(stacked_ext, 'tensor', axis=2, tiled=True)  32.6 us
    unnamed x1, blocking collectives  15.8 us
    psum x1, blocking collectives, body(): lax.psum((group_total(pre_both, group_size), group_total(pre_both * pre_b...  14.6 us
    all_gather x1, blocking collectives, body(): lax.all_gather(stacked_ext[0], 'tensor', axis=1, tiled=True)  14.1 us
    conv_general_dilated x5, matrix products, conv_rows(): lax.conv_general_dilated(inputs, kernel, (1, 1), ((0, 0), (1, 1)), dimens...  13.3 us
    psum x1, blocking collectives, body(): lax.psum((group_total(gnorm, group_size), group_total(gnorm * centered_po...  12.8 us
  transfers between devices with their start and end apart: 8, of which 3 were waited for; matrix products, arithmetic and copies ran while one was open for 1% of the time, Pallas kernels for 0%

commit v1 on v0

--- a/solution.py
+++ b/solution.py
@@ -162,7 +162,8 @@
     dpred_ext = with_halo(dpred, (("space", 2),), 1)
     head_local = kernel_grad(hidden_ext[0], dpred)
     head_local = head_local.transpose(2, 3, 1, 0).reshape(9, latent_chans, chan_local)
-    grad_w2 = lax.psum(head_local, ("dp", "space"))
+    blocks = lax.all_gather(head_local, ("dp", "space"))
+    grad_w2 = jnp.sum(blocks, axis=0)
     dhidden = conv_rows(dpred_ext, flip_kernel(w2_policy))
     normed_policy = normed[0]
     centered_policy = centered[0]

time: 518 us -> 454 us (0.88)
  blocking collectives: 381 us -> 183 us
  waiting for transfers between devices: 37.4 us -> 171 us
    psum x1 -> x0, blocking collectives: 249 us -> none  [body(): grad_w2 = lax.psum(head_local, ('dp', 'space'))]
    unnamed x3, waiting for transfers between devices: 0.03 us -> 135 us
    all_gather x0 -> x1, blocking collectives: none -> 50.7 us  [body(): blocks = lax.all_gather(head_local, ('dp', 'space'))]
  transfers between devices with their start and end apart: 8 -> 8, of which waited for: 3 -> 4; matrix products, arithmetic and copies ran while one was open for 1% -> 1% of each run, Pallas kernels for 0% -> 0%
where the time goes in v1:
time: 454 us
  blocking collectives  183 us (40%)
  waiting for transfers between devices  171 us (38%)
  local copies, waits for them, and re-layouts  33.2 us (7%)
  matrix products  22.4 us (5%)
  between operations  20.5 us (5%)
  other arithmetic  15.4 us (3%)
  starting transfers between devices  8.29 us (2%)
    unnamed x3, waiting for transfers between devices  135 us
    psum x1, blocking collectives, body(): errors = lax.psum(squares, ('space', 'tensor'))  64.8 us
    all_gather x1, blocking collectives, body(): blocks = lax.all_gather(head_local, ('dp', 'space'))  50.7 us
    all_gather x1, waiting for transfers between devices, body(): block_in = lax.all_gather(stacked_ext, 'tensor', axis=2, tiled=True)  31.3 us
    unnamed x1, blocking collectives  15.8 us
    psum x1, blocking collectives, body(): lax.psum((group_total(pre_both, group_size), group_total(pre_both * pre_b...  14.6 us
    all_gather x1, blocking collectives, body(): lax.all_gather(stacked_ext[0], 'tensor', axis=1, tiled=True)  14.1 us
    conv_general_dilated x5, matrix products, conv_rows(): lax.conv_general_dilated(inputs, kernel, (1, 1), ((0, 0), (1, 1)), dimens...  13.3 us
  transfers between devices with their start and end apart: 8, of which 4 were waited for; matrix products, arithmetic and copies ran while one was open for 1% of the time, Pallas kernels for 0%

profile of v1, /device:TPU:8, one launch (start us, length us, event | category | flops | bytes accessed | tf_op | source)
XLA Modules:
  0.0 453.6 jit_solution(16331643061071486178)
XLA Ops:
  7.3 1.2 copy_dynamic-update-slice_fusion.1
  8.5 1.1 copy_dynamic-update-slice_fusion
  9.8 1.7 collective-permute-start
  11.5 1.3 collective-permute-start.1
  12.8 3.1 collective-permute-done.1
  16.0 1.5 pad_maximum_fusion.2
  18.9 0.6 dynamic-slice.1
  19.5 0.6 dynamic-slice.5
  20.8 0.2 fusion.70
  21.1 1.9 slice.99
  22.9 31.3 %all-gather.3.cloned.1.call-done = bf16[2,2,320,6,128]{4,1,3,0,2:T(2,128)(2,1)} async-done(((bf16[2,2,80,6,128]{4,1,3,0,2:T(2,128)(2,1)}), bf16[2,2,320,6,128]{4,1,3,0,2:T(2,128)(2,1)}) %all-gather.3.cloned.1.call-update) | async-done | bytes 1966096 | tf_op jit(solution)/shard_map/all_gather | solution.py:109
  54.3 3.3 slice_bitcast_fusion.1
  57.6 3.8 copy.156
  61.4 1.0 pad.clone
  62.6 1.4 fusion.2
  64.0 2.1 fusion.13
  66.1 0.2 copy.125
  66.3 2.0 copy.157
  68.3 1.0 pad.2.clone
  69.5 1.4 fusion.3
  70.9 2.1 fusion.19
  73.0 0.2 copy.129
  73.3 1.1 copy_bitcast_fusion.1
  74.4 0.2 copy.131
  74.6 0.2 copy.132
  74.8 0.4 fusion.43
  75.2 14.6 %all-reduce.4 = (f32[2,2,8]{2,1,0:T(2,128)S(1)}, f32[2,2,8]{2,1,0:T(2,128)S(1)}) all-reduce(f32[2,2,8]{2,1,0:T(2,128)S(1)} %get-tuple-element.4, f32[2,2,8]{2,1,0:T(2,128)S(1)} %get-tuple-element.3), channel_id=1, replica_groups=mesh['dp'=8,'space'=8,'tensor'=4] {'space'}, use_global_device_ids=true, to_apply=%region_3.0 | all-reduce | flops 64 | bytes 512 | tf_op jit(solution)/shard_map/psum | solution.py:116
  90.1 2.5 fusion.25
  92.6 0.2 fusion.66
  92.8 1.3 collective-permute-start.2
  94.1 1.3 collective-permute-start.3
  95.4 14.1 %all-gather = bf16[1,2,320,6,128]{4,1,3,0,2:T(2,128)(2,1)S(1)} all-gather(bf16[1,2,80,6,128]{4,1,3,0,2:T(2,128)(2,1)S(1)} %copy-done.2), channel_id=2, replica_groups=mesh['dp'=8,'space'=8,'tensor'=4] {'tensor'}, dimensions={2}, use_global_device_ids=true | all-gather | bytes 1228800 | tf_op jit(solution)/shard_map/all_gather | solution.py:185
  109.5 1.4 pad_maximum_fusion
  110.9 1.3 slice_bitcast_fusion.4
  112.2 0.4 pad.6
  112.7 4.0 convolution_select_fusion.1
  116.7 1.1 copy.139
  117.9 1.4 pad.4
  119.5 4.7 %convolution_select_fusion.2 = f32[4,16,17,4]{1,3,2,0:T(4,128)} fusion(bf16[3,3,4,80]{3,2,1,0:T(4,128)(2,1)} %bitcast.168, bf16[80,6,2,7,2]{0,3,2,4,1:T(8,128)(2,1)S(1)} %slice.94, bf16[80,6,2,8,17]{0,3,2,4,1:T(8,128)(2,1)S(1)} %copy.134, pred[16,17]{0,1:T(8,128)(4,1)} %constant.66), kind=kOutput, calls=%fused_computation.19 | convolution fusion | flops 7146752 | bytes 311440 | tf_op jit(solution)/shard_map/conv_general_dilated | solution.py:39
  124.2 1.1 copy.135
  125.4 15.8 %all-reduce.5 = (f32[2,4,4,128]{3,2,0,1:T(4,128)S(1)}, f32[2,4,4,128]{3,2,0,1:T(4,128)S(1)}) all-reduce(f32[2,4,4,128]{3,2,0,1:T(4,128)S(1)} %copy.136, f32[2,4,4,128]{3,2,0,1:T(4,128)S(1)} %copy.140), channel_id=3, replica_groups=mesh['dp'=8,'space'=8,'tensor'=4] {'tensor'}, use_global_device_ids=true, to_apply=%region_4.5.clone | all-reduce | flops 8192 | bytes 65536
  141.1 1.4 multiply_reduce_fusion.2
  142.6 3.2 copy.141
  145.8 64.8 %psum.37 = f32[2,2]{1,0:T(2,128)S(1)} all-reduce(f32[2,2]{1,0:T(2,128)S(1)} %pad_maximum_fusion.5), channel_id=1, replica_groups=mesh['dp'=8,'space'=8,'tensor'=4] {'space','tensor'}, use_global_device_ids=true, to_apply=%region_8.9 | all-reduce | flops 4 | bytes 32 | tf_op jit(solution)/shard_map/psum | solution.py:145
  210.6 0.7 fusion.69
  213.9 0.7 broadcast_multiply_fusion.3
  214.6 1.4 multiply_convert_fusion.2
  216.0 10.2 %all_gather.14 = bf16[2,4,4,128]{3,2,0,1:T(4,128)(2,1)S(1)} all-gather(bf16[2,1,4,128]{3,2,0,1:T(4,128)(2,1)S(1)} %multiply_convert_fusion.2), channel_id=1, replica_groups=mesh['dp'=8,'space'=8,'tensor'=4] {'tensor'}, dimensions={1}, use_global_device_ids=true | all-gather | bytes 10240 | tf_op jit(solution)/shard_map/all_gather | solution.py:161
  226.2 1.3 collective-permute-start.4
  227.5 1.3 collective-permute-start.5
  228.9 0.3 copy.150
  229.3 1.2 collective-permute-done.5
  230.9 0.2 copy.146
  231.2 0.4 convolution_select_fusion
  231.6 0.2 copy.147
  231.9 0.9 copy-done.1
  232.8 2.1 fusion.63
  235.3 12.8 %all-reduce.3 = (f32[2,8]{1,0:T(2,128)S(1)}, f32[2,8]{1,0:T(2,128)S(1)}) all-reduce(f32[2,8]{1,0:T(2,128)S(1)} %reduce_sum.86, f32[2,8]{1,0:T(2,128)S(1)} %reduce_sum.83), channel_id=1, replica_groups=mesh['dp'=8,'space'=8,'tensor'=4] {'space'}, use_global_device_ids=true, to_apply=%region_14.15 | all-reduce | flops 32 | bytes 256 | tf_op jit(solution)/shard_map/psum | solution.py:177
  248.4 7.2 %fusion.22 = f32[3,3,80,320]{2,3,1,0:T(8,128)} fusion(bf16[1,2,320,6,128]{2,1,4,3,0:T(2,128)(2,1)} %copy.141, f32[2,80,4,128]{1,0,3,2:T(2,128)} %get-tuple-element.15, f32[2,2,80,4,128]{2,1,4,3,0:T(2,128)S(1)} %get-tuple-element.18, f32[2,80]{1,0:T(2,128)S(1)} %mul.129, f32[2,80]{1,0:T(2,128)S(1)} %sub.65, f32[2,80]{1,0:T(2,128)S(1)} %mul.114), kind=kOutput, calls=%fused_computation.16 | convolution fusion | flops 469811200 | bytes 2759680 | tf_op jit(solution)/shard_map/transpose | solution.py:186
  255.6 1.6 fusion.44
  257.2 50.7 %all_gather.15 = f32[64,9,4,80]{3,2,1,0:T(4,128)S(1)} all-gather(f32[1,9,4,80]{3,2,1,0:T(4,128)S(1)} %bitcast.159), channel_id=1, replica_groups=mesh['dp'=8,'space'=8,'tensor'=4] {'dp','space'}, dimensions={0}, use_global_device_ids=true | all-gather | bytes 748800 | tf_op jit(solution)/shard_map/all_gather | solution.py:165
  307.9 0.9 reduce_sum.87
  308.8 135.3 %all-reduce.8.cloned.1.call-done = f32[9,80,320]{1,2,0:T(8,128)} async-done(((f32[9,80,320]{1,2,0:T(8,128)}), f32[9,80,320]{1,2,0:T(8,128)}) %all-reduce.8.cloned.1.call-update) | async-done | bytes 921616
  444.1 1.5 constant_dynamic-slice_fusion
  (92 shorter events, 2.6 us)
Async XLA Ops:
  7.2 56.8 %copy-start = (bf16[9,80,320]{2,1,0:T(8,128)(2,1)S(1)}, bf16[9,80,320]{2,1,0:T(8,128)(2,1)}, u32[]{:S(2)}) copy-start(bf16[9,80,320]{2,1,0:T(8,128)(2,1)} %param.20) | copy-start | bytes 1382404
  7.2 11.7 %copy-start.15 = (u32[256]{0:T(256)S(1)}, u32[256]{0:T(256)}, u32[]{:S(2)}) copy-start(u32[256]{0:T(256)} %constant.73) | copy-start | bytes 3076
  7.2 12.3 %copy-start.14 = (u32[256]{0:T(256)S(1)}, u32[256]{0:T(256)}, u32[]{:S(2)}) copy-start(u32[256]{0:T(256)} %constant.81) | copy-start | bytes 3076
  7.2 13.5 %copy-start.4 = (f32[80]{0:T(128)S(1)}, f32[80]{0:T(128)}, u32[]{:S(2)}) copy-start(f32[80]{0:T(128)} %param.24) | copy-start | bytes 964
  7.2 13.5 %copy-start.8 = (f32[80]{0:T(128)S(1)}, f32[80]{0:T(128)}, u32[]{:S(2)}) copy-start(f32[80]{0:T(128)} %param.26) | copy-start | bytes 964
  7.2 13.5 %copy-start.10 = (f32[80]{0:T(128)S(1)}, f32[80]{0:T(128)}, u32[]{:S(2)}) copy-start(f32[80]{0:T(128)} %param.25) | copy-start | bytes 964
  7.2 13.5 %copy-start.9 = (f32[80]{0:T(128)S(1)}, f32[80]{0:T(128)}, u32[]{:S(2)}) copy-start(f32[80]{0:T(128)} %param.27) | copy-start | bytes 964
  7.2 13.6 %copy-start.6 = (f32[80]{0:T(128)S(1)}, f32[80]{0:T(128)}, u32[]{:S(2)}) copy-start(f32[80]{0:T(128)} %param.22) | copy-start | bytes 964
  7.3 13.6 %copy-start.7 = (f32[80]{0:T(128)S(1)}, f32[80]{0:T(128)}, u32[]{:S(2)}) copy-start(f32[80]{0:T(128)} %param.23) | copy-start | bytes 964
  7.3 13.6 %copy-start.3 = (f32[1000,80]{0,1:T(8,128)S(1)}, f32[1000,80]{0,1:T(8,128)}, u32[]{:S(2)}) copy-start(f32[1000,80]{0,1:T(8,128)} %param.30) | copy-start | bytes 960004
  7.3 47.0 %all-gather.3.cloned.1.call-start = ((), (), s32[]{:S(2)}) async-start(), calls=%async_computation | async-start | bytes 2457600 | tf_op jit(solution)/shard_map/all_gather | solution.py:109
  9.8 3.1 collective-permute-start
  11.5 4.4 collective-permute-start.1
  17.5 426.6 %all-reduce.8.cloned.1.call-start = ((), (), s32[]{:S(2)}) async-start(), calls=%async_computation.1 | async-start | bytes 2949120
  62.5 1.4 copy-start.16
  69.5 1.4 copy-start.11
  90.1 5.3 %copy-start.2 = (bf16[1,2,80,6,128]{4,1,3,0,2:T(2,128)(2,1)S(1)}, bf16[1,2,80,6,128]{4,1,3,0,2:T(2,128)(2,1)}, u32[]{:S(2)}) copy-start(bf16[1,2,80,6,128]{4,1,3,0,2:T(2,128)(2,1)} %slice.99) | copy-start | bytes 737284
  92.8 16.7 %collective-permute-start.2 = (bf16[2,2,80,1,128]{2,1,4,3,0:T(2,128)(2,1)S(1)}, bf16[2,2,80,1,128]{2,1,4,3,0:T(2,128)(2,1)S(1)}, u32[]{:S(2)}, u32[]{:S(2)}) collective-permute-start(bf16[2,2,80,1,128]{2,1,4,3,0:T(2,128)(2,1)S(1)} %get-tuple-element.23), channel_id=1, source_target_pairs={{0,4},{4,8},{8,12},{12,16},{16,20},{20,24},{24,28},{1,5},{5,9},{9,... | collective-permute-start | bytes 245768 | tf_op jit(solution)/shard_map/ppermute | solution.py:20
  94.1 15.4 %collective-permute-start.3 = (bf16[2,2,80,1,128]{2,1,4,3,0:T(2,128)(2,1)S(1)}, bf16[2,2,80,1,128]{2,1,4,3,0:T(2,128)(2,1)S(1)}, u32[]{:S(2)}, u32[]{:S(2)}) collective-permute-start(bf16[2,2,80,1,128]{2,1,4,3,0:T(2,128)(2,1)S(1)} %get-tuple-element.24), channel_id=1, source_target_pairs={{4,0},{8,4},{12,8},{16,12},{20,16},{24,20},{28,24},{5,1},{9,5},{13... | collective-permute-start | bytes 245768 | tf_op jit(solution)/shard_map/ppermute | solution.py:22
  110.9 1.8 copy-start.12
  142.6 88.6 %copy-start.13 = (bf16[9,4,80]{2,1,0:T(4,128)(2,1)S(1)}, bf16[9,4,80]{2,1,0:T(4,128)(2,1)}, u32[]{:S(2)}) copy-start(bf16[9,4,80]{2,1,0:T(4,128)(2,1)} %param.28) | copy-start | bytes 17284
  142.6 88.6 %copy-start.17 = (pred[16,17]{0,1:T(8,128)(4,1)S(1)}, pred[16,17]{0,1:T(8,128)(4,1)}, u32[]{:S(2)}) copy-start(pred[16,17]{0,1:T(8,128)(4,1)} %constant.66) | copy-start | bytes 820
  226.2 3.1 collective-permute-start.4
  227.5 3.1 collective-permute-start.5
  231.6 1.2 copy-start.1
  231.6 1.2 copy-start.5
Sparse Core Ops, SparseCore 0:
  17.6 36.5 all-gather.2
  255.8 188.2 all-reduce.7
